TPU v7x, 128 devices: a whole 4x4x4 slice. The times are simulated.
128 devices in a mesh: replica: 2 (over z_lo), shard: 64 (over x, y, z_hi, core).
Axes of the slice: x: 4, y: 4, z: 4 (z_hi: 2, z_lo: 2; z = z_hi * 2 + z_lo), core: 2. Of those that a mesh axis runs over, the one named last changes fastest.
Arguments:
- tokens: bfloat16 [131072, 960], P(('replica', 'shard')), may hold values from -6 to 6
- cotangent: bfloat16 [131072, 960], P(('replica', 'shard')), may hold values from -6 to 6
- query_weight: bfloat16 [960, 960], P('shard'), may hold values from -1 to 1
- key_weight: bfloat16 [960, 320], P('shard'), may hold values from -1 to 1
- value_weight: bfloat16 [960, 320], P('shard'), may hold values from -0.1875 to 0.1875
- w_gate: bfloat16 [960, 2560], P('shard'), may hold values from -0.1875 to 0.1875
- w_up: bfloat16 [960, 2560], P('shard'), may hold values from -0.1875 to 0.1875
- output_weight: bfloat16 [960, 960], P(None, 'shard'), may hold values from -0.75 to 0.75
- w_down: bfloat16 [2560, 960], P(None, 'shard'), may hold values from -0.125 to 0.125
- norm_attn: bfloat16 [960], P('shard'), may hold values from 0.5 to 1.5
- norm_ffn: bfloat16 [960], P('shard'), may hold values from 0.5 to 1.5
Outputs:
- output: bfloat16 [131072, 960], P(('replica', 'shard'))
- grad_tokens: float32 [131072, 960], P(('replica', 'shard'))
- grad_query: float32 [960, 960], P('shard')
- grad_key: float32 [960, 320], P('shard')
- grad_value: float32 [960, 320], P('shard')
- grad_gate: float32 [960, 2560], P('shard')
- grad_up: float32 [960, 2560], P('shard')
- grad_out: float32 [960, 960], P(None, 'shard')
- grad_down: float32 [2560, 960], P(None, 'shard')
- grad_norm_attn: float32 [960], P('shard')
- grad_norm_ffn: float32 [960], P('shard')
All inputs are finite; a program needn't handle non-finite values.
Results may differ from a plain program's by a relative error of at most 0.018.
The roundings to bfloat16 on the way count: a program that leaves them out, or rounds other values in their place, can miss the bound.
Values may be sent and summed in bfloat16 or wider, within the bound.
A program may use at most 256 MiB of HBM per device.

v0:
```python
import functools
import math

import jax
import jax.numpy as jnp
import numpy as np
from jax import lax
from jax.experimental import pallas as pl
from jax.experimental.pallas import tpu as pltpu
from jax.sharding import PartitionSpec as P

F32, BF16 = jnp.float32, jnp.bfloat16
MESH = pl.DeviceIdType.MESH
ANY = pl.BlockSpec(memory_space=pl.ANY)
VMEM = pl.BlockSpec(memory_space=pltpu.VMEM)
WIDTH = 960
D = 1024
T = 1024
SEQ = 512
NQ = 1664
NA, NB, NC, BLOCKS, FB = 1792, 1024, 1536, 5, 512
EARLY = 3
NE, NL = NB + EARLY * NC, (BLOCKS - EARLY) * NC
L0 = 2304
L1 = NL + NB - L0
E0 = NB + NC
E1 = NE - E0
A0 = 1024
A1 = NA - A0
EPS = 1e-05
SCALE = 0.125
LOG2E = math.log2(math.e)
VLIM = 60 * 1024 * 1024


def dot(a, b):
    return lax.dot_general(a, b, (((1,), (0,)), ((), ())), preferred_element_type=F32)


def dot_nt(a, b):
    return lax.dot_general(a, b, (((1,), (1,)), ((), ())), preferred_element_type=F32)


def dot_tn(a, b):
    return lax.dot_general(a, b, (((0,), (0,)), ((), ())), preferred_element_type=F32)


def span(i, n):
    return pl.ds(pl.multiple_of(i * n, n), n)


def rope_tables():
    rates = np.exp(np.arange(32) * (-2.0 * math.log(10000.0) / 64))
    angles = np.arange(SEQ)[:, None] * rates[None, :]
    cos, sin = np.cos(angles), np.sin(angles)
    cosine = np.concatenate([cos] * 4, axis=1).astype(np.float32)
    sine = np.concatenate([-sin, sin] * 2, axis=1).astype(np.float32)
    return cosine, sine


def swapped(t):
    lane = lax.broadcasted_iota(jnp.int32, t.shape, 1)
    return jnp.where((lane & 63) < 32, pltpu.roll(t, 96, 1), pltpu.roll(t, 32, 1))


def tile(p):
    return span(p, 128)


def low_half(shape):
    return lax.broadcasted_iota(jnp.int32, shape, 1) < 64


def spread_matrix():
    row = lax.broadcasted_iota(jnp.int32, (WIDTH, D), 0)
    col = lax.broadcasted_iota(jnp.int32, (WIDTH, D), 1)
    hit = (row == 15 * (col >> 4) + (col & 15)) & ((col & 15) < 15)
    return jnp.where(hit, 1.0, 0.0).astype(BF16)


def place():
    r, s = lax.axis_index("replica"), lax.axis_index("shard")
    return s // 16, (s // 4) % 4, ((s // 2) % 2) * 2 + r, s % 2


def device(x, y, z, c):
    return (z % 2, ((x * 4 + y) * 2 + z // 2) * 2 + c)


def peers():
    x, y, z, c = place()
    along = {
        "x": [device((x + d) % 4, y, z, c) for d in (1, 2, 3)],
        "y": [device(x, (y + d) % 4, z, c) for d in (1, 2, 3)],
        "z": [device(x, y, (z + d) % 4, c) for d in (1, 2, 3)],
    }
    return along, device(x, y, z, 1 - c)


def meet():
    along, other = peers()
    barrier = pltpu.get_barrier_semaphore()
    for d in (*along["x"], *along["y"], *along["z"], other):
        pl.semaphore_signal(barrier, inc=1, device_id=d, device_id_type=MESH)
    pl.semaphore_wait(barrier, 10)


def remote(src, dst, ss, rs, k, to):
    return pltpu.make_async_remote_copy(
        src_ref=src, dst_ref=dst, send_sem=ss.at[k], recv_sem=rs.at[k], device_id=to, device_id_type=MESH
    )


def parts(n):
    tiles = n // 256
    widths = [128 * (tiles // 3), 128 * (tiles // 3), 128 * (tiles - 2 * (tiles // 3))]
    return [(0, widths[0]), (2 * widths[0], widths[1]), (2 * widths[0] + 2 * widths[1], widths[2])]


def half_of(offset, width, k):
    return pl.ds(pl.multiple_of(offset + k * width, 128), width)


SEMS = 30
GATHER_ORDER = ("yxz", "zyx", "xzy")
SCATTER_ORDER = ("zxy", "xyz", "yzx")


class Gather:
    def __init__(self, own, full, ss, rs, n):
        x, y, z, c = place()
        zh, zl = z // 2, z % 2
        along, other = peers()
        self.local, self.stages = [], [[], [], []]
        k = 3
        for (off, w), order in zip(parts(n), GATHER_ORDER):
            mine = half_of(off, w, zl)
            self.local.append(pltpu.make_async_copy(own.at[:, mine], full.at[x, y, zh, c, :, mine], ss.at[len(self.local)]))
            for i, axis in enumerate(order):
                have = order[:i]
                every = slice(None)
                at = (
                    every if "x" in have else x,
                    every if "y" in have else y,
                    every if "z" in have else zh,
                    c,
                    every,
                    pl.ds(off, 2 * w) if "z" in have else mine,
                )
                for to in along[axis]:
                    src = own.at[:, mine] if i == 0 else full.at[at]
                    self.stages[i].append(remote(src, full.at[at], ss, rs, k, to))
                    k += 1
        w = full.at[:, :, :, c]
        self.core = remote(w, w, ss, rs, k, other)

    def move(self, done, begin):
        for d in done:
            d.wait()
        for d in begin:
            d.start()

    def follow(self, i):
        for k in range(0, 9, 3):
            self.move(self.stages[i][k : k + 3], self.stages[i + 1][k : k + 3])

    def s0(self):
        self.move([], self.local + self.stages[0])

    def s1(self):
        self.move(self.local, [])
        self.follow(0)

    def s2(self):
        self.follow(1)

    def s3(self):
        self.move(self.stages[2], [self.core])

    def s4(self):
        self.move([self.core], [])


def gather_sems():
    return [pltpu.SemaphoreType.DMA((SEMS + 1,)), pltpu.SemaphoreType.DMA((SEMS + 1,))]


def extent(left, w):
    return tuple([4] * ("x" in left) + [4] * ("y" in left) + [2] * ("z" in left) + [16, 2 * w if "z" in left else w])


def slot(left, axis, t, off, w):
    every = slice(None)
    cols = pl.ds(off, 2 * w) if "z" in left else every
    if axis == "z":
        cols = half_of(off, w, t % 2)
    at = [every] * ("x" in left) + [every] * ("y" in left) + [every] * ("z" in left)
    lead = [a for a in "xyz" if a in left]
    at[lead.index(axis)] = t // 2 if axis == "z" else t
    return (*at, every, cols)


LANDING, LOCAL = 13, 8


def landing(n):
    one, two, three = [], [], []
    for (_, w), order in zip(parts(n), SCATTER_ORDER):
        one.append(pltpu.VMEM((3, *extent(order[1:], w)), BF16))
        two.append(pltpu.VMEM((3, *extent(order[2:], w)), BF16))
        three.append(pltpu.VMEM((3, 16, w), F32))
    sems = [pltpu.SemaphoreType.DMA((SEMS,)), pltpu.SemaphoreType.DMA((SEMS,))]
    return [pltpu.VMEM((4, 4, 2, 16, n), BF16), *one, *two, *three, pltpu.VMEM((16, n // 2), F32), *sems]


def local(n):
    two, three = [], []
    for (_, w), order in zip(parts(n), SCATTER_ORDER):
        two.append(pltpu.VMEM(extent(order[1:], w), BF16))
        three.append(pltpu.VMEM(extent(order[2:], w), F32))
    return [pltpu.VMEM((4, 4, 2, 16, n), BF16), *two, *three, pltpu.VMEM((16, n // 2), F32)]


def within(loc, n):
    wide = lambda ref, w: ref.at[(*[slice(None)] * (len(ref.shape) - 1), pl.ds(0, w))]
    widths = [2 * w if "z" in order[i:] else w for i in (1, 2) for (_, w), order in zip(parts(n), SCATTER_ORDER)]
    return [wide(ref, w) for ref, w in zip(loc, [n, *widths, n // 2])]


class Scatter:
    def __init__(self, part, out, land, loc, n):
        x, y, z, c = place()
        self.own = part.at[:, :, :, c]
        self.at, self.out, self.parts = {"x": x, "y": y, "z": z}, out, parts(n)
        along, other = peers()
        self.r0, self.r4, ss, rs = land[0], *land[10:]
        self.p1, self.p4 = loc[0], loc[7]
        self.took = [land[1:4], land[4:7], land[7:10]]
        self.held = [[self.p1] * 3, loc[1:4], loc[4:7]]
        self.local = pltpu.make_async_copy(part.at[:, :, :, c], self.p1, ss.at[0])
        self.core = remote(part.at[:, :, :, 1 - c], self.r0, ss, rs, 1, other)
        self.sends, k = [[], [], []], 2
        for i in range(3):
            for q, order in enumerate(SCATTER_ORDER):
                for d in (1, 2, 3):
                    axis = order[i]
                    src = self.held[i][q].at[self.index(q, i, (self.at[axis] + d) % 4)]
                    self.sends[i].append(remote(src, self.took[i][q].at[d - 1], ss, rs, k, along[axis][d - 1]))
                    k += 1
        self.rep = remote(self.p4, self.r4, ss, rs, k, device(x, y, z + 1 - 2 * (z % 2), c))

    def index(self, q, i, t):
        off, w = self.parts[q]
        order = SCATTER_ORDER[q]
        return slot(order[i:], order[i], t, off if i == 0 else 0, w)

    def total(self, i, to):
        for q, order in enumerate(SCATTER_ORDER):
            own = self.held[i][q].at[self.index(q, i, self.at[order[i]])]
            took = self.took[i][q]
            lead = own.shape[:-2]

            def add(j, own=own, took=took, q=q):
                value = own[j].astype(F32)
                for k in range(3):
                    value += took[(k, *j)].astype(F32)
                to(q, j, value)

            if len(lead) == 2:

                def turn(a, _, add=add, lead=lead):
                    for b in range(lead[1]):
                        add((a, b))
                    return 0

                lax.fori_loop(0, lead[0], turn, 0)
            elif len(lead) == 1:
                for a in range(lead[0]):
                    add((a,))
            else:
                add(())

    def s0(self):
        self.local.start()
        self.core.start()

    def s1(self):
        self.local.wait()
        self.core.wait()
        self.merge(self.p1)

    def s0_vmem(self):
        self.core.start()

    def s1_vmem(self):
        self.core.wait()
        self.merge(self.own)

    def merge(self, own):
        def add(i, _):
            a, b = i // 4, i % 4
            self.p1[a, b] = (own[a, b].astype(F32) + self.r0[a, b].astype(F32)).astype(BF16)
            return 0

        lax.fori_loop(0, 16, add, 0)
        for d in self.sends[0]:
            d.start()

    def stage(self, i):
        for d in self.sends[i]:
            d.wait()

        def to(q, j, value):
            ref = self.held[i + 1][q]
            ref[j] = value.astype(ref.dtype)

        self.total(i, to)
        for d in self.sends[i + 1]:
            d.start()

    def s2(self):
        self.stage(0)

    def s3(self):
        self.stage(1)

    def s4(self):
        for d in self.sends[2]:
            d.wait()

        def to(q, j, value):
            off, w = self.parts[q]
            self.p4[:, off // 2 : off // 2 + w] = value

        self.total(2, to)
        self.rep.start()

    def s5(self):
        self.rep.wait()
        k = self.at["z"] % 2
        for off, w in self.parts:
            self.out[:, half_of(off, w, k)] = self.p4[:, off // 2 : off // 2 + w]
            self.out[:, half_of(off, w, 1 - k)] = self.r4[:, off // 2 : off // 2 + w]


def run(plan, i):
    for at, steps in plan.items():

        @pl.when(i == at)
        def _():
            for step in steps:
                step()


def attend_kernel(tok_hbm, cot_hbm, cos_ref, sin_ref, a, e0, e1, xp_ref, cp_ref, nrm_ref, qt_ref, ho_ref, lt_ref, gains_ref, fa, f0, f1,
                  tok, cot, spread, full, kx, vx, lse, bias, sem, *sems):
    meet()
    first = Gather(a, full, sems[0], sems[1], NA)
    c0, c1 = Gather(e0, f0, sems[2], sems[3], E0), Gather(e1, f1, sems[4], sems[5], E1)
    first.s0()
    reads = [pltpu.make_async_copy(tok_hbm, tok, sem.at[0]), pltpu.make_async_copy(cot_hbm, cot, sem.at[1])]
    for r in reads:
        r.start()
    spread[...] = spread_matrix()
    row = lax.broadcasted_iota(jnp.int32, (256, 256), 0)
    col = lax.broadcasted_iota(jnp.int32, (256, 256), 1)
    bias[...] = jnp.where(col <= row, 0.0, -1e30)
    ho_ref[...] = jnp.zeros_like(ho_ref)
    lse[...] = jnp.zeros_like(lse)
    first.s1()
    c0.s0()
    for r in reads:
        r.wait()

    def widen(src, to):
        def turn(i, _):
            r = span(i, 512)
            to[r, :] = dot_tn(src[:, r], spread[...]).astype(BF16)
            return 0

        lax.fori_loop(0, 2, turn, 0)

    widen(tok, xp_ref)
    first.s2()
    c0.s1()
    c1.s0()
    widen(cot, cp_ref)
    first.s3()
    c0.s2()
    c1.s1()
    first.s4()
    keep = pltpu.make_async_copy(full, fa, sem.at[0])
    keep.start()
    a_ref = full.reshape(D, NA)
    gains_ref[...] = jnp.transpose(a_ref[:, NQ - 128 : NQ].astype(F32))[64:72, :]
    gain = gains_ref[0:1, :]

    def project(i, _):
        r = span(i, 512)
        x = xp_ref[r, :].astype(F32)
        recip = lax.rsqrt(jnp.sum(x * x, axis=1, keepdims=True) * (1.0 / WIDTH) + EPS)
        normed = (x * recip * gain).astype(BF16)
        nrm_ref[r, :] = normed
        for at in range(0, NQ, 512):
            width = min(512, NQ - at)
            q = dot(normed, a_ref[:, at : at + width])
            for t in range(at, at + width, 128):
                v = q[:, t - at : t - at + 128]
                if t < 1280:
                    v = v * cos_ref[...] + swapped(v) * sin_ref[...]
                qt_ref[r, t : t + 128] = v.astype(BF16)
        run({0: [c1.s2]}, i)
        return 0

    lax.fori_loop(0, 2, project, 0)
    split_heads(qt_ref, kx, vx)

    def head(h, _):
        p, g = h // 2, h // 3
        u = 2 * g + h - 2 * p
        jobs = [(slice(SEQ * s + 256 * b, SEQ * s + 256 * b + 256), slice(SEQ * s, SEQ * s + 256 * b + 256)) for s in range(2) for b in range(2)]
        scores = [dot_nt(qt_ref[rows, tile(p)], kx[u, keys, :]) * (SCALE * LOG2E) for rows, keys in jobs]
        softs, stats = [], []
        for sc in scores:
            n = sc.shape[1]
            last = sc[:, n - 256 :] + bias[...]
            sc = last if n == 256 else jnp.concatenate([sc[:, : n - 256], last], axis=1)
            top = jnp.max(sc, axis=1, keepdims=True)
            ex = jnp.exp2(sc - top)
            total = jnp.sum(ex, axis=1, keepdims=True)
            softs.append((ex * (1.0 / total)).astype(BF16))
            stats.append(top + jnp.log2(total))
        outs = [dot(soft, vx[u, keys, :]) for soft, (_, keys) in zip(softs, jobs)]
        lane = lax.broadcasted_iota(jnp.int32, (256, 128), 1)
        for (rows, _), o, stat in zip(jobs, outs, stats):
            ho_ref[rows, tile(p)] = ho_ref[rows, tile(p)] + o.astype(BF16)
            lse[rows, :] = jnp.where(lane == h, stat, lse[rows, :])
        run({1: [c0.s3], 10: [c1.s3], 12: [c0.s4]}, h)
        return 0

    lax.fori_loop(0, 15, head, 0)
    lt_ref[...] = jnp.transpose(lse[...])[:16, :].reshape(16, 1, T)
    keep.wait()
    c1.s4()


def split_heads(qt_ref, kx, vx):
    low = low_half((T, 128))
    for g in range(5):
        for to, unit in ((kx, 15 + g), (vx, 20 + g)):
            at = 128 * (unit // 2)
            v = qt_ref[:, at : at + 128].astype(F32)
            turned = pltpu.roll(v, 64, 1)
            at_low, at_high = (v, turned) if unit % 2 == 0 else (turned, v)
            to[2 * g] = jnp.where(low, at_low, 0.0).astype(BF16)
            to[2 * g + 1] = jnp.where(low, 0.0, at_high).astype(BF16)


def attend(tok, cot, cosine, sine, a, e0, e1):
    shape = jax.ShapeDtypeStruct
    return pl.pallas_call(
        attend_kernel,
        out_shape=[
            shape((T, D), BF16),
            shape((T, D), BF16),
            shape((T, D), BF16),
            shape((T, NQ), BF16),
            shape((T, D), BF16),
            shape((16, 1, T), F32),
            shape((8, D), F32),
            shape((4, 4, 2, 2, 16, NA), BF16),
            shape((4, 4, 2, 2, 16, E0), BF16),
            shape((4, 4, 2, 2, 16, E1), BF16),
        ],
        in_specs=[ANY] * 2 + [VMEM] * 2 + [ANY] * 3,
        out_specs=[VMEM] * 7 + [ANY] * 3,
        scratch_shapes=[
            pltpu.VMEM((WIDTH, T), BF16),
            pltpu.VMEM((WIDTH, T), BF16),
            pltpu.VMEM((WIDTH, D), BF16),
            pltpu.VMEM((4, 4, 2, 2, 16, NA), BF16),
            pltpu.VMEM((10, T, 128), BF16),
            pltpu.VMEM((10, T, 128), BF16),
            pltpu.VMEM((T, 128), F32),
            pltpu.VMEM((256, 256), F32),
            pltpu.SemaphoreType.DMA((2,)),
            *gather_sems() * 3,
        ],
        compiler_params=pltpu.CompilerParams(collective_id=0, has_side_effects=True, vmem_limit_bytes=VLIM),
        name="attend",
    )(tok, cot, cosine, sine, a, e0, e1)


def ffn_kernel(xp, cp, gains, ho, f0, f1, c_own, hid, gheads_ref, gnorm_ref, oc_ref, outp_hbm, gl_hbm, fc,
               b_full, acc, gacc, nrm, w, act, ggu, stage, wsem, gsem, *scratch):
    meet()
    gather = Gather(c_own, fc, scratch[0], scratch[1], NL)
    lands, loc = scratch[2 : 2 + LANDING], scratch[2 + LANDING :]
    reduction = lambda j: Scatter(stage, oc_ref.at[j], [ref.at[j] for ref in lands], loc, NC)
    gain = gains[1:2, :]
    get_b = pltpu.make_async_copy(f0.at[:, :, :, :, :, :NB], b_full, gsem)
    get_b.start()

    def fetch(b, begin):
        slot = jnp.asarray(b) % 2

        @pl.when(b == 0)
        def _():
            d = pltpu.make_async_copy(f0.at[:, :, :, :, :, NB:], w.at[slot], wsem.at[slot])
            d.start() if begin else d.wait()

        @pl.when((b > 0) & (b < EARLY))
        def _():
            cols = pl.ds(pl.multiple_of(NC * jnp.clip(b - 1, 0, EARLY - 2), 128), NC)
            d = pltpu.make_async_copy(f1.at[:, :, :, :, :, cols], w.at[slot], wsem.at[slot])
            d.start() if begin else d.wait()

        @pl.when(b >= EARLY)
        def _():
            cols = pl.ds(pl.multiple_of(NC * jnp.maximum(b - EARLY, 0), 128), NC)
            d = pltpu.make_async_copy(fc.at[:, :, :, :, :, cols], w.at[slot], wsem.at[slot])
            d.start() if begin else d.wait()

    gather.s0()
    fetch(0, True)
    get_b.wait()
    b_ref = b_full.reshape(D, NB)

    def first(i, _):
        r = span(i, 512)
        h = xp[r, :].astype(F32) + dot_nt(ho[r, :], b_ref[...])
        hid[r, :] = h
        acc[r, :] = h
        recip = lax.rsqrt(jnp.sum(h * h, axis=1, keepdims=True) * (1.0 / WIDTH) + EPS)
        nrm[r, :] = (h * recip * gain).astype(BF16)
        gacc[r, :] = jnp.zeros((512, D), F32)
        run({0: [gather.s1], 1: [gather.s2]}, i)
        return 0

    lax.fori_loop(0, 2, first, 0)

    def when_chunk(b, ahead, name):
        @pl.when((b >= ahead) & (b < ahead + EARLY))
        def _():
            getattr(reduction(b - ahead), name)()

    def block(b, _):
        wv = w.at[b % 2].reshape(D, NC)
        fetch(b, False)

        @pl.when(b < BLOCKS - 1)
        def _():
            fetch(b + 1, True)

        when_chunk(b, 1, "s0_vmem")
        when_chunk(b, 3, "s3")
        when_chunk(b, 4, "s5")

        @pl.when(b == 1)
        def _():
            gather.s3()

        def rows(i, _):
            r = span(i, 512)
            pre = dot(nrm[r, :], wv[:, : 2 * FB])
            ga = dot(cp[r, :], wv[:, 2 * FB :])
            gate, up = pre[:, :FB], pre[:, FB:]
            sig = 0.5 * jnp.tanh(0.5 * gate) + 0.5
            silu = gate * sig
            act_b = (silu * up).astype(BF16)
            act[r, :] = act_b
            ggu[r, :FB] = (ga * up * (sig + silu * (1.0 - sig))).astype(BF16)
            ggu[r, FB:] = (ga * silu).astype(BF16)
            acc[r, :] += dot_nt(act_b, wv[:, 2 * FB :])
            gacc[r, :] += dot_nt(ggu[r, :], wv[:, : 2 * FB])
            return 0

        lax.fori_loop(0, 2, rows, 0)
        when_chunk(b, 2, "s2")
        when_chunk(b, 1, "s1_vmem")
        when_chunk(b, 3, "s4")

        @pl.when(b == 1)
        def _():
            gather.s4()

        @pl.when(b == BLOCKS - 1)
        def _():
            pltpu.make_async_copy(stage, gl_hbm.at[:, :, :, :, :, :NC], gsem).wait()

        def weights(i, _):
            r = span(i, 512)
            k = pl.ds(pl.multiple_of(2 * i, 2), 2)
            to = lambda v: v.astype(BF16).reshape(2, 4, 2, 2, 16, v.shape[1])
            stage[k, :, :, :, :, : 2 * FB] = to(dot_tn(nrm[:, r], ggu[...]))
            stage[k, :, :, :, :, 2 * FB :] = to(dot_tn(cp[:, r], act[...]))
            return 0

        lax.fori_loop(0, 2, weights, 0)

        @pl.when(b >= EARLY)
        def _():
            cols = pl.ds(pl.multiple_of(NC * jnp.maximum(b - EARLY, 0), 128), NC)
            pltpu.make_async_copy(stage, gl_hbm.at[:, :, :, :, :, cols], gsem).start()

        return 0

    lax.fori_loop(0, BLOCKS, block, 0)
    reduction(1).s5()
    reduction(2).s3()
    gnorm_ref[...] = jnp.zeros_like(gnorm_ref)
    out_stage = w.at[0].reshape(D, NC).at[:, :D]

    def last(i, _):
        r = span(i, 256)
        out_stage[r, :] = acc[r, :].astype(BF16)
        h, gn = hid[r, :], gacc[r, :]
        recip = lax.rsqrt(jnp.sum(h * h, axis=1, keepdims=True) * (1.0 / WIDTH) + EPS)
        gnorm_ref[...] += jnp.sum(gn * h * recip, axis=0, keepdims=True)
        scaled = gn * gain
        mean = jnp.sum(scaled * h, axis=1, keepdims=True) * (1.0 / WIDTH)
        gh = cp[r, :].astype(F32) + recip * scaled - h * (recip * recip * recip * mean)
        hid[r, :] = gh
        nrm[r, :] = gh.astype(BF16)
        return 0

    lax.fori_loop(0, 4, last, 0)
    reduction(2).s4()
    put_out = pltpu.make_async_copy(out_stage, outp_hbm, wsem.at[0])
    put_out.start()
    pltpu.make_async_copy(stage, gl_hbm.at[:, :, :, :, :, :NC], gsem).wait()

    def out_grad(i, _):
        r = span(i, 512)
        k = pl.ds(pl.multiple_of(2 * i, 2), 2)
        stage[k, :, :, :, :, :NB] = dot_tn(nrm[:, r], ho[...]).astype(BF16).reshape(2, 4, 2, 2, 16, NB)
        return 0

    lax.fori_loop(0, 2, out_grad, 0)
    put_gb = pltpu.make_async_copy(stage.at[:, :, :, :, :, :NB], gl_hbm.at[:, :, :, :, :, NL:], gsem)
    put_gb.start()

    def heads(i, _):
        r = span(i, 512)
        gheads_ref[r, :] = dot(nrm[r, :], b_ref[...]).astype(BF16)
        return 0

    lax.fori_loop(0, 2, heads, 0)
    reduction(2).s5()
    put_out.wait()
    put_gb.wait()


def many(shapes, k):
    vmem = lambda s: pltpu.VMEM((k, *s.shape), s.dtype)
    return [vmem(s) if i < len(shapes) - 2 else pltpu.SemaphoreType.DMA((k, SEMS)) for i, s in enumerate(shapes)]


def ffn(xp, cp, gains, ho, f0, f1, c_own):
    shape = jax.ShapeDtypeStruct
    return pl.pallas_call(
        ffn_kernel,
        out_shape=[
            shape((T, D), F32),
            shape((T, D), BF16),
            shape((1, D), F32),
            shape((EARLY, 16, NC), F32),
            shape((T, D), BF16),
            shape((4, 4, 2, 2, 16, NL + NB), BF16),
            shape((4, 4, 2, 2, 16, NL), BF16),
        ],
        in_specs=[VMEM] * 4 + [ANY] * 3,
        out_specs=[VMEM] * 4 + [ANY] * 3,
        scratch_shapes=[
            pltpu.VMEM((4, 4, 2, 2, 16, NB), BF16),
            pltpu.VMEM((T, D), F32),
            pltpu.VMEM((T, D), F32),
            pltpu.VMEM((T, D), BF16),
            pltpu.VMEM((2, 4, 4, 2, 2, 16, NC), BF16),
            pltpu.VMEM((T, FB), BF16),
            pltpu.VMEM((T, 2 * FB), BF16),
            pltpu.VMEM((4, 4, 2, 2, 16, NC), BF16),
            pltpu.SemaphoreType.DMA((2,)),
            pltpu.SemaphoreType.DMA,
            *gather_sems(),
            *many(landing(NC), EARLY),
            *local(NC),
        ],
        compiler_params=pltpu.CompilerParams(collective_id=1, has_side_effects=True, vmem_limit_bytes=VLIM),
        name="ffn",
    )(xp, cp, gains, ho, f0, f1, c_own)


def back_kernel(qt_ref, ho_ref, gheads_ref, lt_ref, cos_ref, sin_ref, gains, nrm, xp, gnf, gl, fa, gh_hbm, outp_hbm,
                o0_ref, o1_ref, oa0_ref, oa1_ref, gtok_hbm, out_hbm, full, dt_ref, gsum, cols_ref, isem, osem, *scratch):
    meet()
    chunks, at = [], 0
    sources = [(gl.at[:, :, :, :, :, :L0], o0_ref, L0), (gl.at[:, :, :, :, :, L0:], o1_ref, L1)]
    k = LANDING + LOCAL
    for i, (src, out, n) in enumerate(sources):
        chunks.append(Scatter(src, out, scratch[k * i : k * i + LANDING], scratch[k * i + LANDING : k * i + k], n))
    c0, c1 = chunks
    loc0, loc1 = scratch[LANDING:k], scratch[k + LANDING : 2 * k]
    scratch = scratch[2 * k :]
    c0.s0()
    c1.s0()
    get_a = pltpu.make_async_copy(fa, full, isem.at[0])
    get_a.start()

    def phase_one(kx, vx, dq, dk, dv, bias):
        split_heads(qt_ref, kx, vx)
        dq[...] = jnp.zeros_like(dq)
        dk[...] = jnp.zeros_like(dk)
        dv[...] = jnp.zeros_like(dv)
        row = lax.broadcasted_iota(jnp.int32, (256, 256), 0)
        col = lax.broadcasted_iota(jnp.int32, (256, 256), 1)
        bias[...] = jnp.where(row <= col, 0.0, -1e30)

        def head(h, _):
            p, g = h // 2, h // 3
            par = h - 2 * p
            u = 2 * g + par
            lane = lax.broadcasted_iota(jnp.int32, (SEQ, 128), 1)
            own = (lane // 64) == par
            ones = jnp.ones((8, 128), BF16)
            c = SCALE * LOG2E
            for s in range(2):
                seq = slice(SEQ * s, SEQ * s + SEQ)
                q, do = qt_ref[seq, tile(p)], gheads_ref[seq, tile(p)]
                q_own = jnp.where(own, q, jnp.zeros_like(q))
                do_own = jnp.where(own, do, jnp.zeros_like(do))
                prod = do_own.astype(F32) * ho_ref[seq, tile(p)].astype(F32)
                high = prod.astype(BF16)
                rest = (prod - high.astype(F32)).astype(BF16)
                off = (dot_nt(ones, high) + dot_nt(ones, rest))[:1, :]
                lse = lt_ref[h, :, seq]
                k0, k1 = kx[u, SEQ * s : SEQ * s + 256, :], kx[u, SEQ * s + 256 : SEQ * s + 512, :]
                v0, v1 = vx[u, SEQ * s : SEQ * s + 256, :], vx[u, SEQ * s + 256 : SEQ * s + 512, :]
                st0, st1 = dot_nt(k0, q), dot_nt(k1, q[256:])
                gp0, gp1 = dot_nt(v0, do), dot_nt(v1, do[256:])
                t0 = st0 * c - lse
                e0 = jnp.exp2(jnp.concatenate([t0[:, :256] + bias[...], t0[:, 256:]], axis=1))
                e1 = jnp.exp2(st1 * c - lse[:, 256:] + bias[...])
                ds0 = (e0 * (gp0 - off)).astype(BF16)
                ds1 = (e1 * (gp1 - off[:, 256:])).astype(BF16)
                dv0, dv1 = dot(e0.astype(BF16), do_own), dot(e1.astype(BF16), do_own[256:])
                dk0, dk1 = dot(ds0, q_own), dot(ds1, q_own[256:])
                dq0 = dot_tn(ds0, k0)
                dq1 = dot_tn(ds1, k1)
                lo, hi = slice(SEQ * s, SEQ * s + 256), slice(SEQ * s + 256, SEQ * s + 512)
                dv[g, lo, :] += dv0
                dv[g, hi, :] += dv1
                dk[g, lo, :] += dk0
                dk[g, hi, :] += dk1
                dq[p, lo, :] += dq0[:256]
                dq[p, hi, :] += dq0[256:] + dq1
            run({1: [c0.s1], 3: [c1.s1], 6: [c0.s2], 8: [c0.s3], 9: [c1.s2], 10: [c0.s4], 11: [c1.s3], 12: [c0.s5], 13: [c1.s4]}, h)
            return 0

        lax.fori_loop(0, 15, head, 0)

        def finish(i, _):
            r = span(i, 256)
            half = span(i % 2, 256)
            cosine, sine = cos_ref[half, :], sin_ref[half, :]
            low = low_half((256, 128))
            fold = lambda ref, g: ref[g, r, :] + pltpu.roll(ref[g, r, :], 64, 1)
            tiles = [dq[p, r, :] for p in range(7)]
            tiles.append(jnp.where(low, dq[7, r, :], fold(dk, 0)))
            tiles.append(jnp.where(low, fold(dk, 1), fold(dk, 2)))
            tiles.append(jnp.where(low, fold(dk, 3), fold(dk, 4)))
            for t, v in enumerate(tiles):
                v = v * SCALE
                dt_ref[r, 128 * t : 128 * t + 128] = (v * cosine - swapped(v) * sine).astype(BF16)
            dt_ref[r, 1280:1408] = jnp.where(low, fold(dv, 0), fold(dv, 1)).astype(BF16)
            dt_ref[r, 1408:1536] = jnp.where(low, fold(dv, 2), fold(dv, 3)).astype(BF16)
            dt_ref[r, 1536:1664] = jnp.where(low, fold(dv, 4), 0.0).astype(BF16)
            return 0

        lax.fori_loop(0, 4, finish, 0)

    pl.run_scoped(
        phase_one,
        pltpu.VMEM((10, T, 128), BF16),
        pltpu.VMEM((10, T, 128), BF16),
        pltpu.VMEM((8, T, 128), F32),
        pltpu.VMEM((5, T, 128), F32),
        pltpu.VMEM((5, T, 128), F32),
        pltpu.VMEM((256, 256), F32),
    )
    get_a.wait()
    a_ref = full.reshape(D, NA)
    gain = gains[0:1, :]
    gsum[...] = jnp.zeros_like(gsum)
    gsum[1:2, :] = gnf[...]

    def phase_two(gn_ref, gtok, out, spread, gh, outp, ga0, ga1):
        get_gh = lambda i: pltpu.make_async_copy(gh_hbm.at[span(i, 256), :], gh.at[i % 2], isem.at[i % 2])
        get_out = pltpu.make_async_copy(outp_hbm, outp, osem.at[0])
        get_gh(0).start()
        get_out.start()
        d0 = Scatter(ga0, oa0_ref, scratch[:LANDING], within(loc0, A0), A0)
        d1 = Scatter(ga1, oa1_ref, scratch[LANDING:], within(loc1, A1), A1)
        to = lambda v: v.astype(BF16).reshape(2, 4, 2, 2, 16, v.shape[1])

        def weights0(i, _):
            ga0[pl.ds(pl.multiple_of(2 * i, 2), 2)] = to(dot_tn(nrm[:, span(i, 512)], dt_ref[:, :A0]))
            return 0

        lax.fori_loop(0, 2, weights0, 0)
        d0.s0_vmem()
        c1.s5()

        def normed(i, _):
            r = span(i, 512)
            gn = dot_nt(dt_ref[r, :], a_ref[:, :NQ])
            gn_ref[r, :] = gn
            x = xp[r, :].astype(F32)
            recip = lax.rsqrt(jnp.sum(x * x, axis=1, keepdims=True) * (1.0 / WIDTH) + EPS)
            gsum[0:1, :] += jnp.sum(gn * x * recip, axis=0, keepdims=True)
            run({1: [d0.s1_vmem]}, i)
            return 0

        lax.fori_loop(0, 2, normed, 0)
        cols = jnp.transpose(jnp.concatenate([gsum[...], jnp.zeros((120, D), F32)], axis=0))
        cols_ref[...] = pltpu.roll(cols, 64, 1)

        def weights1(i, _):
            r = span(i, 512)
            kk = pl.ds(pl.multiple_of(2 * i, 2), 2)
            g = dot_tn(nrm[:, r], dt_ref[:, A0:])
            edge = jnp.where(low_half((512, 128)), g[:, NQ - A0 - 128 :], cols_ref[r, :])
            ga1[kk, :, :, :, :, : NQ - A0 - 128] = to(g[:, : NQ - A0 - 128])
            ga1[kk, :, :, :, :, NQ - A0 - 128 : NQ - A0] = to(edge)
            ga1[kk, :, :, :, :, NQ - A0 :] = jnp.zeros((2, 4, 2, 2, 16, NA - NQ), BF16)
            return 0

        lax.fori_loop(0, 2, weights1, 0)
        d1.s0_vmem()
        spread[...] = spread_matrix()
        get_out.wait()
        d0.s2()
        d1.s1_vmem()

        def tokens(i, _):
            r = span(i, 256)
            get_gh(i).wait()

            @pl.when(i < 3)
            def _():
                get_gh(i + 1).start()

            x = xp[r, :].astype(F32)
            recip = lax.rsqrt(jnp.sum(x * x, axis=1, keepdims=True) * (1.0 / WIDTH) + EPS)
            scaled = gn_ref[r, :] * gain
            mean = jnp.sum(scaled * x, axis=1, keepdims=True) * (1.0 / WIDTH)
            gt = gh[i % 2] + recip * scaled - x * (recip * recip * recip * mean)
            high = gt.astype(BF16)
            mid = (gt - high.astype(F32)).astype(BF16)
            gtok[:, r] = dot_nt(spread[...], high) + dot_nt(spread[...], mid)
            out[:, r] = dot_nt(spread[...], outp[r, :]).astype(BF16)
            run({0: [d0.s3], 1: [d0.s4], 2: [d1.s2, d0.s5], 3: [d1.s3]}, i)
            return 0

        lax.fori_loop(0, 4, tokens, 0)
        puts = [pltpu.make_async_copy(gtok, gtok_hbm, osem.at[0]), pltpu.make_async_copy(out, out_hbm, osem.at[1])]
        for p in puts:
            p.start()
        d1.s4()
        d1.s5()
        for p in puts:
            p.wait()

    pl.run_scoped(
        phase_two,
        pltpu.VMEM((T, D), F32),
        pltpu.VMEM((WIDTH, T), F32),
        pltpu.VMEM((WIDTH, T), BF16),
        pltpu.VMEM((WIDTH, D), BF16),
        pltpu.VMEM((2, 256, D), F32),
        pltpu.VMEM((T, D), BF16),
        pltpu.VMEM((4, 4, 2, 2, 16, A0), BF16),
        pltpu.VMEM((4, 4, 2, 2, 16, A1), BF16),
    )


def back(qt, ho, gheads, lt, cosine, sine, gains, nrm, xp, gnf, gl, fa, gh, outp):
    shape = jax.ShapeDtypeStruct
    return pl.pallas_call(
        back_kernel,
        out_shape=[
            shape((16, L0), F32),
            shape((16, L1), F32),
            shape((16, A0), F32),
            shape((16, A1), F32),
            shape((WIDTH, T), F32),
            shape((WIDTH, T), BF16),
        ],
        in_specs=[VMEM] * 10 + [ANY] * 4,
        out_specs=[VMEM] * 4 + [ANY] * 2,
        scratch_shapes=[
            pltpu.VMEM((4, 4, 2, 2, 16, NA), BF16),
            pltpu.VMEM((T, NQ), BF16),
            pltpu.VMEM((8, D), F32),
            pltpu.VMEM((D, 128), F32),
            pltpu.SemaphoreType.DMA((2,)),
            pltpu.SemaphoreType.DMA((2,)),
            *landing(L0),
            *local(L0),
            *landing(L1),
            *local(L1),
            *landing(A0),
            *landing(A1),
        ],
        compiler_params=pltpu.CompilerParams(collective_id=2, has_side_effects=True, vmem_limit_bytes=VLIM),
        name="back",
    )(qt, ho, gheads, lt, cosine, sine, gains, nrm, xp, gnf, gl, fa, gh, outp)


def shards(tokens, cotangent, wq, wk, wv, w_gate, w_up, wo, w_down, norm_attn, norm_ffn):
    pad = lambda a, n: jnp.pad(a, ((0, 1), (0, n - a.shape[1])))
    a = pad(jnp.concatenate([wq, wk, wv, norm_attn[:, None], norm_ffn[:, None]], axis=1), NA)
    down = w_down.T
    blocks = [jnp.concatenate([w[:, FB * i : FB * i + FB] for w in (w_gate, w_up, down)], axis=1) for i in range(BLOCKS)]
    e0 = pad(jnp.concatenate([jnp.pad(wo.T, ((0, 0), (0, NB - WIDTH))), blocks[0]], axis=1), E0)
    e1 = pad(jnp.concatenate(blocks[1:EARLY], axis=1), E1)
    late = pad(jnp.concatenate(blocks[EARLY:], axis=1), NL)
    cosine, sine = rope_tables()
    xp, cp, nrm, qt, ho, lt, gains, fa, f0, f1 = attend(tokens.T, cotangent.T, cosine, sine, a, e0, e1)
    gh, gheads, gnf, early, outp, gl, _ = ffn(xp, cp, gains, ho, f0, f1, late)
    l0, l1, a0, a1, grad_tokens, output = back(qt, ho, gheads, lt, cosine, sine, gains, nrm, xp, gnf, gl, fa, gh, outp)
    sa = jnp.concatenate([a0, a1], axis=1)
    left = jnp.concatenate([l0, l1], axis=1)[:15]
    pieces = [early[i, :15] for i in range(EARLY)] + [left[:, NC * i : NC * i + NC] for i in range(BLOCKS - EARLY)]
    join = lambda k: jnp.concatenate([v[:, FB * k : FB * k + FB] for v in pieces], axis=1)
    return (
        output.T,
        grad_tokens.T,
        sa[:15, :960],
        sa[:15, 960:1280],
        sa[:15, 1280:1600],
        join(0),
        join(1),
        left[:, NL : NL + WIDTH].T,
        join(2).T,
        sa[:15, 1600],
        sa[:15, 1601],
    )


def solution(mesh):
    rows = P(("replica", "shard"), None)
    first, second, one = P("shard", None), P(None, "shard"), P("shard")
    in_specs = (rows, rows, first, first, first, first, first, second, second, one, one)
    out_specs = (rows, rows, first, first, first, first, first, second, second, one, one)
    return jax.shard_map(shards, mesh=mesh, in_specs=in_specs, out_specs=out_specs, check_vma=False)
```

profile of v0, /device:TPU:0, one launch (start us, length us, event | category | flops | bytes accessed | tf_op | source)
XLA Modules:
  0.0 274.3 jit_solution(6430544545629729566)
XLA Ops:
  0.6 0.7 copy.26
  1.4 0.8 copy.27
  2.1 0.9 concatenate.27
  3.7 0.7 constant_dynamic-update-slice_fusion.11
  4.4 0.7 constant_dynamic-update-slice_fusion.10
  5.1 0.7 constant_dynamic-update-slice_fusion.9
  5.9 0.8 constant_dynamic-update-slice_fusion.8
  6.6 0.8 constant_dynamic-update-slice_fusion.7
  7.4 0.8 constant_dynamic-update-slice_fusion.6
  8.1 0.7 pad.23.c_own
  8.8 0.8 fusion.3
  10.2 0.7 pad.22.e1
  10.9 68.7 %attend.1 = (bf16[1024,1024]{1,0:T(8,128)(2,1)}, bf16[1024,1024]{1,0:T(8,128)(2,1)}, bf16[1024,1024]{1,0:T(8,128)(2,1)}, bf16[1024,1664]{1,0:T(8,128)(2,1)}, bf1...) custom-call(bf16[960,1024]{1,0:T(8,128)(2,1)} %bitcast.19, ...), custom_call_target="tpu_custom_call" | custom-call | tf_op jit(solution)/shard_map/attend/pallas_call | solution.py:461
  79.6 94.1 %ffn.1 = (f32[1024,1024]{1,0:T(8,128)}, bf16[1024,1024]{1,0:T(8,128)(2,1)}, f32[1,1024]{1,0:T(1,128)}, f32[3,16,1536]{2,1,0:T(8,128)}, bf16[1024,1024]{1,0:T(8,1...) custom-call(bf16[1024,1024]{1,0:T(8,128)(2,1)} %get-tuple-element.35.xp, ...), custom_call_target="tpu_custom_call" | custom-call | tf_op jit(solution)/shard_map/ffn/pallas_call | solution.py:661
  173.6 88.9 %back.1 = (f32[16,2304]{1,0:T(8,128)}, f32[16,1792]{1,0:T(8,128)}, f32[16,1024]{1,0:T(8,128)}, f32[16,768]{1,0:T(8,128)}, f32[960,1024]{1,0:T(8,128)}, /*index=5*/bf16[960,1024]{1,0:T(8,128)(2,1)}) custom-call(bf16[1024,1664]{1,0:T(8,128)(2,1)} %get-tuple-element.33.qt_ref, bf16[1024,1024]{1,0:T(8,128)(2,1)} %get-tuple-element.34.ho.ho_ref, ...), custom_call_target="tpu_custom_call" | custom-call | tf_op jit(solution)/shard_map/back/pallas_call | solution.py:889
  262.5 1.6 slice_reduce_fusion
  264.1 1.4 fusion.4
  265.5 1.5 slice_bitcast_fusion.3
  267.1 0.8 constant_dynamic-update-slice_fusion.18
  267.8 0.8 constant_dynamic-update-slice_fusion.23
  268.7 0.9 constant_dynamic-update-slice_fusion.22
  269.6 1.3 copy.53
  270.9 0.8 copy-done
  271.7 1.9 copy.54
  (20 shorter events, 2.0 us)
Async XLA Ops:
  173.6 93.4 %copy-start.2 = (f32[3,16,1536]{2,1,0:T(8,128)S(1)}, f32[3,16,1536]{2,1,0:T(8,128)}, u32[]{:S(2)}) copy-start(f32[3,16,1536]{2,1,0:T(8,128)} %get-tuple-element.52) | copy-start | bytes 884740
  262.5 7.1 %copy-start.1 = (bf16[960,1024]{1,0:T(8,128)(2,1)S(1)}, bf16[960,1024]{1,0:T(8,128)(2,1)}, u32[]{:S(2)}) copy-start(bf16[960,1024]{1,0:T(8,128)(2,1)} %get-tuple-element.48) | copy-start | bytes 5898244
  268.7 5.0 %copy-start.5 = (f32[15,2560]{1,0:T(8,128)}, f32[15,2560]{1,0:T(8,128)S(1)}, u32[]{:S(2)}) copy-start(f32[15,2560]{1,0:T(8,128)S(1)} %get-tuple-element.108) | copy-start | bytes 460804
  268.7 5.0 %copy-start.6 = (f32[15,2560]{1,0:T(8,128)}, f32[15,2560]{1,0:T(8,128)S(1)}, u32[]{:S(2)}) copy-start(f32[15,2560]{1,0:T(8,128)S(1)} %get-tuple-element.107) | copy-start | bytes 460804
  268.7 3.0 %copy-start = (f32[960,1024]{1,0:T(8,128)S(1)}, f32[960,1024]{1,0:T(8,128)}, u32[]{:S(2)}) copy-start(f32[960,1024]{1,0:T(8,128)} %get-tuple-element.49) | copy-start | bytes 11796484
  269.6 4.0 %copy-start.4 = (f32[15,2560]{1,0:T(8,128)}, f32[15,2560]{1,0:T(8,128)S(1)}, u32[]{:S(2)}) copy-start(f32[15,2560]{1,0:T(8,128)S(1)} %constant_dynamic-update-slice_fusion.22) | copy-start | bytes 460804
  271.7 1.9 copy-start.3
where the time goes:
time: 275 us; the launch traced here: 274 us
  Pallas kernels  252 us (92%)
  local copies, waits for them, and re-layouts  18.9 us (7%)
  other arithmetic  2.99 us (1%)
    pallas_call x1, Pallas kernels, ffn(): pl.pallas_call(ffn_kernel, out_shape=[shape((T, D), F32), shape((T, D), B...  94.1 us
    pallas_call x1, Pallas kernels, back(): pl.pallas_call(back_kernel, out_shape=[shape((16, L0), F32), shape((16, L...  88.9 us
    pallas_call x1, Pallas kernels, attend(): pl.pallas_call(attend_kernel, out_shape=[shape((T, D), BF16), shape((T, D...  68.7 us
    unnamed x26, local copies, waits for them, and re-layouts  9.21 us

commit v1 on v0

--- a/solution.py
+++ b/solution.py
@@ -17,14 +17,15 @@
 D = 1024
 T = 1024
 SEQ = 512
-NQ = 1664
+K_UNIT, V_UNIT = 16, 22
 NA, NB, NC, BLOCKS, FB = 1792, 1024, 1536, 5, 512
+AHEAD = 2
 EARLY = 3
-NE, NL = NB + EARLY * NC, (BLOCKS - EARLY) * NC
+NL = (BLOCKS - EARLY) * NC
 L0 = 2304
 L1 = NL + NB - L0
-E0 = NB + NC
-E1 = NE - E0
+E0, E1 = NB + NC, NC
+F0, F1 = NC, 2 * NC
 A0 = 1024
 A1 = NA - A0
 EPS = 1e-05
@@ -352,15 +353,52 @@
                 step()
 
 
-def attend_kernel(tok_hbm, cot_hbm, cos_ref, sin_ref, a, e0, e1, xp_ref, cp_ref, nrm_ref, qt_ref, ho_ref, lt_ref, gains_ref, fa, f0, f1,
-                  tok, cot, spread, full, kx, vx, lse, bias, sem, *sems):
+def lay(own, at, raw, start=0, width=None):
+    width = raw.shape[1] if width is None else width
+    own[:15, at : at + width] = raw[:, start : start + width]
+
+
+def lay_blocks(own, at, blocks, gate, up, down):
+    for b in blocks:
+        for raw in (gate, up, down):
+            lay(own, at, raw, FB * b, FB)
+            at += FB
+
+
+def attend_kernel(tok_hbm, cot_hbm, cos_ref, sin_ref, gain_ref, *refs):
+    raw_hbm, refs = refs[:7], refs[7:]
+    xp_ref, cp_ref, nrm_ref, qt_ref, ho_ref, lt_ref, gains_ref, fa, f0, f1, tok, cot, spread, full, kx, vx, lse, bias, a, e0, e1, sem, *refs = refs
+    raw, (rsem, *sems) = refs[:7], refs[7:]
+    wq, wk, wv, wo, gate, up, down = raw
+    loads = [pltpu.make_async_copy(h, v, rsem.at[i]) for i, (h, v) in enumerate(zip(raw_hbm, raw))]
+    for d in loads:
+        d.start()
+    for own in (a, e0, e1):
+        own[...] = jnp.zeros_like(own)
+    diagonal = lax.broadcasted_iota(jnp.int32, (15, 15), 0) == lax.broadcasted_iota(jnp.int32, (15, 15), 1)
+    lane = lax.broadcasted_iota(jnp.int32, (15, 128), 1)
+    edge = jnp.zeros((15, 128), F32)
+    for i in range(2):
+        column = jnp.sum(jnp.where(diagonal, gain_ref[i : i + 1, :].astype(F32), 0.0), axis=1, keepdims=True)
+        edge = jnp.where(lane == 64 + i, column, edge)
     meet()
+    for d in loads[:3]:
+        d.wait()
+    lay(a, 0, wq)
+    lay(a, 64 * K_UNIT, wk)
+    a[:15, NA - 128 :] = edge.astype(BF16)
+    lay(a, 64 * V_UNIT, wv)
     first = Gather(a, full, sems[0], sems[1], NA)
     c0, c1 = Gather(e0, f0, sems[2], sems[3], E0), Gather(e1, f1, sems[4], sems[5], E1)
     first.s0()
     reads = [pltpu.make_async_copy(tok_hbm, tok, sem.at[0]), pltpu.make_async_copy(cot_hbm, cot, sem.at[1])]
     for r in reads:
         r.start()
+    for d in loads[3:]:
+        d.wait()
+    lay(e0, 0, wo)
+    lay_blocks(e0, NB, [0], gate, up, down)
+    lay_blocks(e1, 0, [1], gate, up, down)
     spread[...] = spread_matrix()
     row = lax.broadcasted_iota(jnp.int32, (256, 256), 0)
     col = lax.broadcasted_iota(jnp.int32, (256, 256), 1)
@@ -392,7 +430,7 @@
     keep = pltpu.make_async_copy(full, fa, sem.at[0])
     keep.start()
     a_ref = full.reshape(D, NA)
-    gains_ref[...] = jnp.transpose(a_ref[:, NQ - 128 : NQ].astype(F32))[64:72, :]
+    gains_ref[...] = jnp.transpose(a_ref[:, NA - 128 :].astype(F32))[64:72, :]
     gain = gains_ref[0:1, :]
 
     def project(i, _):
@@ -401,12 +439,12 @@
         recip = lax.rsqrt(jnp.sum(x * x, axis=1, keepdims=True) * (1.0 / WIDTH) + EPS)
         normed = (x * recip * gain).astype(BF16)
         nrm_ref[r, :] = normed
-        for at in range(0, NQ, 512):
-            width = min(512, NQ - at)
+        for at in range(0, NA, 512):
+            width = min(512, NA - at)
             q = dot(normed, a_ref[:, at : at + width])
             for t in range(at, at + width, 128):
                 v = q[:, t - at : t - at + 128]
-                if t < 1280:
+                if t < 64 * V_UNIT:
                     v = v * cos_ref[...] + swapped(v) * sin_ref[...]
                 qt_ref[r, t : t + 128] = v.astype(BF16)
         run({0: [c1.s2]}, i)
@@ -447,7 +485,7 @@
 def split_heads(qt_ref, kx, vx):
     low = low_half((T, 128))
     for g in range(5):
-        for to, unit in ((kx, 15 + g), (vx, 20 + g)):
+        for to, unit in ((kx, K_UNIT + g), (vx, V_UNIT + g)):
             at = 128 * (unit // 2)
             v = qt_ref[:, at : at + 128].astype(F32)
             turned = pltpu.roll(v, 64, 1)
@@ -456,7 +494,7 @@
             to[2 * g + 1] = jnp.where(low, 0.0, at_high).astype(BF16)
 
 
-def attend(tok, cot, cosine, sine, a, e0, e1):
+def attend(tok, cot, cosine, sine, gain, raw):
     shape = jax.ShapeDtypeStruct
     return pl.pallas_call(
         attend_kernel,
@@ -464,7 +502,7 @@
             shape((T, D), BF16),
             shape((T, D), BF16),
             shape((T, D), BF16),
-            shape((T, NQ), BF16),
+            shape((T, NA), BF16),
             shape((T, D), BF16),
             shape((16, 1, T), F32),
             shape((8, D), F32),
@@ -472,7 +510,7 @@
             shape((4, 4, 2, 2, 16, E0), BF16),
             shape((4, 4, 2, 2, 16, E1), BF16),
         ],
-        in_specs=[ANY] * 2 + [VMEM] * 2 + [ANY] * 3,
+        in_specs=[ANY] * 2 + [VMEM] * 3 + [ANY] * 7,
         out_specs=[VMEM] * 7 + [ANY] * 3,
         scratch_shapes=[
             pltpu.VMEM((WIDTH, T), BF16),
@@ -483,45 +521,49 @@
             pltpu.VMEM((10, T, 128), BF16),
             pltpu.VMEM((T, 128), F32),
             pltpu.VMEM((256, 256), F32),
+            pltpu.VMEM((16, NA), BF16),
+            pltpu.VMEM((16, E0), BF16),
+            pltpu.VMEM((16, E1), BF16),
             pltpu.SemaphoreType.DMA((2,)),
+            *[pltpu.VMEM(r.shape, BF16) for r in raw],
+            pltpu.SemaphoreType.DMA((7,)),
             *gather_sems() * 3,
         ],
         compiler_params=pltpu.CompilerParams(collective_id=0, has_side_effects=True, vmem_limit_bytes=VLIM),
         name="attend",
-    )(tok, cot, cosine, sine, a, e0, e1)
-
-
-def ffn_kernel(xp, cp, gains, ho, f0, f1, c_own, hid, gheads_ref, gnorm_ref, oc_ref, outp_hbm, gl_hbm, fc,
-               b_full, acc, gacc, nrm, w, act, ggu, stage, wsem, gsem, *scratch):
+    )(tok, cot, cosine, sine, gain, *raw)
+
+
+def ffn_kernel(xp, cp, gains, ho, e0, e1, gate_hbm, up_hbm, down_hbm, hid, gheads_ref, gnorm_ref, oc_ref, outp_hbm, gl_hbm, f0, f1,
+               b_full, acc, gacc, nrm, w, act, ggu, stage, own0, own1, gate, up, down, rsem, wsem, gsem, *scratch):
+    loads = [pltpu.make_async_copy(h, v, rsem.at[i]) for i, (h, v) in enumerate(((gate_hbm, gate), (up_hbm, up), (down_hbm, down)))]
+    for d in loads:
+        d.start()
+    own0[...] = jnp.zeros_like(own0)
+    own1[...] = jnp.zeros_like(own1)
     meet()
-    gather = Gather(c_own, fc, scratch[0], scratch[1], NL)
-    lands, loc = scratch[2 : 2 + LANDING], scratch[2 + LANDING :]
+    for d in loads:
+        d.wait()
+    lay_blocks(own0, 0, [AHEAD], gate, up, down)
+    lay_blocks(own1, 0, range(AHEAD + 1, BLOCKS), gate, up, down)
+    g0, g1 = Gather(own0, f0, scratch[0], scratch[1], F0), Gather(own1, f1, scratch[2], scratch[3], F1)
+    lands, loc = scratch[4 : 4 + LANDING], scratch[4 + LANDING :]
     reduction = lambda j: Scatter(stage, oc_ref.at[j], [ref.at[j] for ref in lands], loc, NC)
     gain = gains[1:2, :]
-    get_b = pltpu.make_async_copy(f0.at[:, :, :, :, :, :NB], b_full, gsem)
+    get_b = pltpu.make_async_copy(e0.at[:, :, :, :, :, :NB], b_full, gsem)
     get_b.start()
 
     def fetch(b, begin):
         slot = jnp.asarray(b) % 2
 
-        @pl.when(b == 0)
-        def _():
-            d = pltpu.make_async_copy(f0.at[:, :, :, :, :, NB:], w.at[slot], wsem.at[slot])
-            d.start() if begin else d.wait()
-
-        @pl.when((b > 0) & (b < EARLY))
-        def _():
-            cols = pl.ds(pl.multiple_of(NC * jnp.clip(b - 1, 0, EARLY - 2), 128), NC)
-            d = pltpu.make_async_copy(f1.at[:, :, :, :, :, cols], w.at[slot], wsem.at[slot])
-            d.start() if begin else d.wait()
-
-        @pl.when(b >= EARLY)
-        def _():
-            cols = pl.ds(pl.multiple_of(NC * jnp.maximum(b - EARLY, 0), 128), NC)
-            d = pltpu.make_async_copy(fc.at[:, :, :, :, :, cols], w.at[slot], wsem.at[slot])
-            d.start() if begin else d.wait()
-
-    gather.s0()
+        for at, src in ((0, e0.at[:, :, :, :, :, NB:]), (1, e1), (2, f0), (3, f1.at[:, :, :, :, :, :NC]), (4, f1.at[:, :, :, :, :, NC:])):
+
+            @pl.when(b == at)
+            def _():
+                d = pltpu.make_async_copy(src, w.at[slot], wsem.at[slot])
+                d.start() if begin else d.wait()
+
+    g0.s0()
     fetch(0, True)
     get_b.wait()
     b_ref = b_full.reshape(D, NB)
@@ -534,7 +576,7 @@
         recip = lax.rsqrt(jnp.sum(h * h, axis=1, keepdims=True) * (1.0 / WIDTH) + EPS)
         nrm[r, :] = (h * recip * gain).astype(BF16)
         gacc[r, :] = jnp.zeros((512, D), F32)
-        run({0: [gather.s1], 1: [gather.s2]}, i)
+        run({0: [g0.s1, g1.s0], 1: [g0.s2, g1.s1]}, i)
         return 0
 
     lax.fori_loop(0, 2, first, 0)
@@ -548,17 +590,10 @@
         wv = w.at[b % 2].reshape(D, NC)
         fetch(b, False)
 
-        @pl.when(b < BLOCKS - 1)
-        def _():
-            fetch(b + 1, True)
-
         when_chunk(b, 1, "s0_vmem")
         when_chunk(b, 3, "s3")
         when_chunk(b, 4, "s5")
-
-        @pl.when(b == 1)
-        def _():
-            gather.s3()
+        run({1: [g0.s4], 2: [g1.s4]}, b)
 
         def rows(i, _):
             r = span(i, 512)
@@ -580,9 +615,11 @@
         when_chunk(b, 1, "s1_vmem")
         when_chunk(b, 3, "s4")
 
-        @pl.when(b == 1)
+        run({0: [g0.s3, g1.s2], 1: [g1.s3]}, b)
+
+        @pl.when(b < BLOCKS - 1)
         def _():
-            gather.s4()
+            fetch(b + 1, True)
 
         @pl.when(b == BLOCKS - 1)
         def _():
@@ -656,7 +693,7 @@
     return [vmem(s) if i < len(shapes) - 2 else pltpu.SemaphoreType.DMA((k, SEMS)) for i, s in enumerate(shapes)]
 
 
-def ffn(xp, cp, gains, ho, f0, f1, c_own):
+def ffn(xp, cp, gains, ho, e0, e1, raw):
     shape = jax.ShapeDtypeStruct
     return pl.pallas_call(
         ffn_kernel,
@@ -667,10 +704,11 @@
             shape((EARLY, 16, NC), F32),
             shape((T, D), BF16),
             shape((4, 4, 2, 2, 16, NL + NB), BF16),
-            shape((4, 4, 2, 2, 16, NL), BF16),
+            shape((4, 4, 2, 2, 16, F0), BF16),
+            shape((4, 4, 2, 2, 16, F1), BF16),
         ],
-        in_specs=[VMEM] * 4 + [ANY] * 3,
-        out_specs=[VMEM] * 4 + [ANY] * 3,
+        in_specs=[VMEM] * 4 + [ANY] * 5,
+        out_specs=[VMEM] * 4 + [ANY] * 4,
         scratch_shapes=[
             pltpu.VMEM((4, 4, 2, 2, 16, NB), BF16),
             pltpu.VMEM((T, D), F32),
@@ -680,22 +718,29 @@
             pltpu.VMEM((T, FB), BF16),
             pltpu.VMEM((T, 2 * FB), BF16),
             pltpu.VMEM((4, 4, 2, 2, 16, NC), BF16),
+            pltpu.VMEM((16, F0), BF16),
+            pltpu.VMEM((16, F1), BF16),
+            *[pltpu.VMEM(r.shape, BF16) for r in raw],
+            pltpu.SemaphoreType.DMA((3,)),
             pltpu.SemaphoreType.DMA((2,)),
             pltpu.SemaphoreType.DMA,
-            *gather_sems(),
+            *gather_sems() * 2,
             *many(landing(NC), EARLY),
             *local(NC),
         ],
         compiler_params=pltpu.CompilerParams(collective_id=1, has_side_effects=True, vmem_limit_bytes=VLIM),
         name="ffn",
-    )(xp, cp, gains, ho, f0, f1, c_own)
-
-
-def back_kernel(qt_ref, ho_ref, gheads_ref, lt_ref, cos_ref, sin_ref, gains, nrm, xp, gnf, gl, fa, gh_hbm, outp_hbm,
-                o0_ref, o1_ref, oa0_ref, oa1_ref, gtok_hbm, out_hbm, full, dt_ref, gsum, cols_ref, isem, osem, *scratch):
+    )(xp, cp, gains, ho, e0, e1, *raw)
+
+
+def back_kernel(qt_ref, ho_ref, gheads_ref, lt_ref, cos_ref, sin_ref, gains, nrm, xp, gnf, early, gl, fa, gh_hbm, outp_hbm,
+                oq, ok, ov, og, ou, od, oo, on, gtok_hbm, out_hbm, full, dt_ref, gsum, cols_ref, left, oa0_ref, oa1_ref, isem, osem, *scratch):
     meet()
-    chunks, at = [], 0
-    sources = [(gl.at[:, :, :, :, :, :L0], o0_ref, L0), (gl.at[:, :, :, :, :, L0:], o1_ref, L1)]
+    chunks = []
+    sources = [
+        (gl.at[:, :, :, :, :, :L0], left.at[:, :L0], L0),
+        (gl.at[:, :, :, :, :, L0:], left.at[:, L0:], L1),
+    ]
     k = LANDING + LOCAL
     for i, (src, out, n) in enumerate(sources):
         chunks.append(Scatter(src, out, scratch[k * i : k * i + LANDING], scratch[k * i + LANDING : k * i + k], n))
@@ -765,16 +810,12 @@
             cosine, sine = cos_ref[half, :], sin_ref[half, :]
             low = low_half((256, 128))
             fold = lambda ref, g: ref[g, r, :] + pltpu.roll(ref[g, r, :], 64, 1)
-            tiles = [dq[p, r, :] for p in range(7)]
-            tiles.append(jnp.where(low, dq[7, r, :], fold(dk, 0)))
-            tiles.append(jnp.where(low, fold(dk, 1), fold(dk, 2)))
-            tiles.append(jnp.where(low, fold(dk, 3), fold(dk, 4)))
-            for t, v in enumerate(tiles):
+            pair = lambda ref, g: jnp.where(low, fold(ref, g), fold(ref, g + 1) if g < 4 else 0.0)
+            for t, v in enumerate([dq[p, r, :] for p in range(8)] + [pair(dk, g) for g in (0, 2, 4)]):
                 v = v * SCALE
                 dt_ref[r, 128 * t : 128 * t + 128] = (v * cosine - swapped(v) * sine).astype(BF16)
-            dt_ref[r, 1280:1408] = jnp.where(low, fold(dv, 0), fold(dv, 1)).astype(BF16)
-            dt_ref[r, 1408:1536] = jnp.where(low, fold(dv, 2), fold(dv, 3)).astype(BF16)
-            dt_ref[r, 1536:1664] = jnp.where(low, fold(dv, 4), 0.0).astype(BF16)
+            for t, g in ((11, 0), (12, 2), (13, 4)):
+                dt_ref[r, 128 * t : 128 * t + 128] = pair(dv, g).astype(BF16)
             return 0
 
         lax.fori_loop(0, 4, finish, 0)
@@ -813,7 +854,7 @@
 
         def normed(i, _):
             r = span(i, 512)
-            gn = dot_nt(dt_ref[r, :], a_ref[:, :NQ])
+            gn = dot_nt(dt_ref[r, :], a_ref[...])
             gn_ref[r, :] = gn
             x = xp[r, :].astype(F32)
             recip = lax.rsqrt(jnp.sum(x * x, axis=1, keepdims=True) * (1.0 / WIDTH) + EPS)
@@ -829,10 +870,9 @@
             r = span(i, 512)
             kk = pl.ds(pl.multiple_of(2 * i, 2), 2)
             g = dot_tn(nrm[:, r], dt_ref[:, A0:])
-            edge = jnp.where(low_half((512, 128)), g[:, NQ - A0 - 128 :], cols_ref[r, :])
-            ga1[kk, :, :, :, :, : NQ - A0 - 128] = to(g[:, : NQ - A0 - 128])
-            ga1[kk, :, :, :, :, NQ - A0 - 128 : NQ - A0] = to(edge)
-            ga1[kk, :, :, :, :, NQ - A0 :] = jnp.zeros((2, 4, 2, 2, 16, NA - NQ), BF16)
+            edge = jnp.where(low_half((512, 128)), g[:, A1 - 128 :], cols_ref[r, :])
+            ga1[kk, :, :, :, :, : A1 - 128] = to(g[:, : A1 - 128])
+            ga1[kk, :, :, :, :, A1 - 128 :] = to(edge)
             return 0
 
         lax.fori_loop(0, 2, weights1, 0)
@@ -867,7 +907,22 @@
         for p in puts:
             p.start()
         d1.s4()
+        at = NL
+        oo[...] = left[:15, at : at + WIDTH]
+        for b in range(BLOCKS):
+            for i, to_ref in enumerate((og, ou, od)):
+                cols = slice(FB * b, FB * b + FB)
+                if b < EARLY:
+                    to_ref[:, cols] = early[b, :15, FB * i : FB * i + FB]
+                else:
+                    at = NC * (b - EARLY) + FB * i
+                    to_ref[:, cols] = left[:15, at : at + FB]
+        oq[...] = oa0_ref[:15, :WIDTH]
         d1.s5()
+        ok[...] = oa1_ref[:15, :320]
+        ov[...] = oa1_ref[:15, 64 * V_UNIT - A0 : 64 * V_UNIT - A0 + 320]
+        edge = jnp.concatenate([oa1_ref[:, A1 - 128 :], jnp.zeros((112, 128), F32)], axis=0)
+        on[...] = jnp.transpose(edge)[64:72, :]
         for p in puts:
             p.wait()
 
@@ -884,25 +939,26 @@
     )
 
 
-def back(qt, ho, gheads, lt, cosine, sine, gains, nrm, xp, gnf, gl, fa, gh, outp):
+def back(qt, ho, gheads, lt, cosine, sine, gains, nrm, xp, gnf, early, gl, fa, gh, outp):
     shape = jax.ShapeDtypeStruct
     return pl.pallas_call(
         back_kernel,
         out_shape=[
-            shape((16, L0), F32),
-            shape((16, L1), F32),
-            shape((16, A0), F32),
-            shape((16, A1), F32),
+            *[shape((15, n), F32) for n in (960, 320, 320, 2560, 2560, 2560, 960)],
+            shape((8, 128), F32),
             shape((WIDTH, T), F32),
             shape((WIDTH, T), BF16),
         ],
-        in_specs=[VMEM] * 10 + [ANY] * 4,
-        out_specs=[VMEM] * 4 + [ANY] * 2,
+        in_specs=[VMEM] * 11 + [ANY] * 4,
+        out_specs=[VMEM] * 8 + [ANY] * 2,
         scratch_shapes=[
             pltpu.VMEM((4, 4, 2, 2, 16, NA), BF16),
-            pltpu.VMEM((T, NQ), BF16),
+            pltpu.VMEM((T, NA), BF16),
             pltpu.VMEM((8, D), F32),
             pltpu.VMEM((D, 128), F32),
+            pltpu.VMEM((16, L0 + L1), F32),
+            pltpu.VMEM((16, A0), F32),
+            pltpu.VMEM((16, A1), F32),
             pltpu.SemaphoreType.DMA((2,)),
             pltpu.SemaphoreType.DMA((2,)),
             *landing(L0),
@@ -914,38 +970,43 @@
         ],
         compiler_params=pltpu.CompilerParams(collective_id=2, has_side_effects=True, vmem_limit_bytes=VLIM),
         name="back",
-    )(qt, ho, gheads, lt, cosine, sine, gains, nrm, xp, gnf, gl, fa, gh, outp)
+    )(qt, ho, gheads, lt, cosine, sine, gains, nrm, xp, gnf, early, gl, fa, gh, outp)
+
+
+def settle_kernel(*refs):
+    n = len(refs) // 2
+    for src, dst in zip(refs[: n - 2], refs[n:]):
+
+        @pl.when(pl.program_id(0) == 0)
+        def _():
+            dst[...] = src[...]
+
+    for src, dst in zip(refs[n - 2 : n], refs[2 * n - 2 :]):
+        dst[...] = src[...]
+
+
+def settle(*results):
+    whole = [pl.BlockSpec(r.shape, lambda i: (0, 0)) for r in results[:-2]]
+    rows = [pl.BlockSpec((WIDTH // 4, T), lambda i: (i, 0))] * 2
+    return pl.pallas_call(
+        settle_kernel,
+        grid=(4,),
+        out_shape=[jax.ShapeDtypeStruct(r.shape, r.dtype) for r in results],
+        in_specs=whole + rows,
+        out_specs=whole + rows,
+        name="settle",
+    )(*results)
 
 
 def shards(tokens, cotangent, wq, wk, wv, w_gate, w_up, wo, w_down, norm_attn, norm_ffn):
-    pad = lambda a, n: jnp.pad(a, ((0, 1), (0, n - a.shape[1])))
-    a = pad(jnp.concatenate([wq, wk, wv, norm_attn[:, None], norm_ffn[:, None]], axis=1), NA)
-    down = w_down.T
-    blocks = [jnp.concatenate([w[:, FB * i : FB * i + FB] for w in (w_gate, w_up, down)], axis=1) for i in range(BLOCKS)]
-    e0 = pad(jnp.concatenate([jnp.pad(wo.T, ((0, 0), (0, NB - WIDTH))), blocks[0]], axis=1), E0)
-    e1 = pad(jnp.concatenate(blocks[1:EARLY], axis=1), E1)
-    late = pad(jnp.concatenate(blocks[EARLY:], axis=1), NL)
     cosine, sine = rope_tables()
-    xp, cp, nrm, qt, ho, lt, gains, fa, f0, f1 = attend(tokens.T, cotangent.T, cosine, sine, a, e0, e1)
-    gh, gheads, gnf, early, outp, gl, _ = ffn(xp, cp, gains, ho, f0, f1, late)
-    l0, l1, a0, a1, grad_tokens, output = back(qt, ho, gheads, lt, cosine, sine, gains, nrm, xp, gnf, gl, fa, gh, outp)
-    sa = jnp.concatenate([a0, a1], axis=1)
-    left = jnp.concatenate([l0, l1], axis=1)[:15]
-    pieces = [early[i, :15] for i in range(EARLY)] + [left[:, NC * i : NC * i + NC] for i in range(BLOCKS - EARLY)]
-    join = lambda k: jnp.concatenate([v[:, FB * k : FB * k + FB] for v in pieces], axis=1)
-    return (
-        output.T,
-        grad_tokens.T,
-        sa[:15, :960],
-        sa[:15, 960:1280],
-        sa[:15, 1280:1600],
-        join(0),
-        join(1),
-        left[:, NL : NL + WIDTH].T,
-        join(2).T,
-        sa[:15, 1600],
-        sa[:15, 1601],
-    )
+    gain = jnp.stack([norm_attn, norm_ffn])
+    ffn_raw = (w_gate, w_up, w_down.T)
+    xp, cp, nrm, qt, ho, lt, gains, fa, e0, e1 = attend(tokens.T, cotangent.T, cosine, sine, gain, (wq, wk, wv, wo.T, *ffn_raw))
+    gh, gheads, gnf, early, outp, gl, _, _ = ffn(xp, cp, gains, ho, e0, e1, ffn_raw)
+    results = back(qt, ho, gheads, lt, cosine, sine, gains, nrm, xp, gnf, early, gl, fa, gh, outp)
+    oq, ok, ov, og, ou, od, oo, on, grad_tokens, output = settle(*results)
+    return output.T, grad_tokens.T, oq, ok, ov, og, ou, oo.T, od.T, on[0, :15], on[1, :15]
 
 
 def solution(mesh):

time: 275 us -> 262 us (0.953)
  local copies, waits for them, and re-layouts: 18.9 us -> 1.27 us
  Pallas kernels: 252 us -> 258 us
    unnamed x26 -> x0, local copies, waits for them, and re-layouts: 9.21 us -> none
    pallas_call x1 -> x2, Pallas kernels: 88.9 us -> 95.7 us  [the longest x1 89.6 us: back(): pl.pallas_call(back_kernel, out_shape=[*[shape((15, n), F32) for n in (96...]
where the time goes in v1:
time: 262 us; the launch traced here: 261 us
  Pallas kernels  258 us (98%)
    pallas_call x1, Pallas kernels, ffn(): pl.pallas_call(ffn_kernel, out_shape=[shape((T, D), F32), shape((T, D), B...  96.5 us
    pallas_call x1, Pallas kernels, back(): pl.pallas_call(back_kernel, out_shape=[*[shape((15, n), F32) for n in (96...  89.6 us
    pallas_call x1, Pallas kernels, attend(): pl.pallas_call(attend_kernel, out_shape=[shape((T, D), BF16), shape((T, D...  66.1 us
    pallas_call x1, Pallas kernels, settle(): pl.pallas_call(settle_kernel, grid=(4,), out_shape=[jax.ShapeDtypeStruct(...  6.11 us

profile of v1, /device:TPU:0, one launch (start us, length us, event | category | flops | bytes accessed | tf_op | source)
XLA Modules:
  0.0 261.4 jit_solution(4326768114785964139)
XLA Ops:
  0.6 1.2 pad_maximum_fusion.gain_ref
  1.8 66.1 %attend.1 = (bf16[1024,1024]{1,0:T(8,128)(2,1)}, bf16[1024,1024]{1,0:T(8,128)(2,1)}, bf16[1024,1024]{1,0:T(8,128)(2,1)}, bf16[1024,1792]{1,0:T(8,128)(2,1)}, bf1...) custom-call(bf16[960,1024]{1,0:T(8,128)(2,1)} %bitcast.14, ...), custom_call_target="tpu_custom_call" | custom-call | tf_op jit(solution)/shard_map/attend/pallas_call | solution.py:499
  67.9 96.5 %ffn.1 = (f32[1024,1024]{1,0:T(8,128)}, bf16[1024,1024]{1,0:T(8,128)(2,1)}, f32[1,1024]{1,0:T(1,128)}, f32[3,16,1536]{2,1,0:T(8,128)}, bf16[1024,1024]{1,0:T(8,1...) custom-call(bf16[1024,1024]{1,0:T(8,128)(2,1)} %get-tuple-element.49, ...), custom_call_target="tpu_custom_call" | custom-call | tf_op jit(solution)/shard_map/ffn/pallas_call | solution.py:698
  164.5 89.6 %back.1 = (f32[15,960]{1,0:T(8,128)}, f32[15,320]{1,0:T(8,128)}, f32[15,320]{1,0:T(8,128)}, f32[15,2560]{1,0:T(8,128)}, f32[15,2560]{1,0:T(8,128)}, /*index=5*/f...) custom-call(bf16[1024,1792]{1,0:T(8,128)(2,1)} %get-tuple-element.47.qt_r, ...), custom_call_target="tpu_custom_call" | custom-call | tf_op jit(solution)/shard_map/back/pallas_call | solution.py:944
  254.0 6.1 %settle.1 = (f32[15,960]{1,0:T(8,128)}, f32[15,320]{1,0:T(8,128)}, f32[15,320]{1,0:T(8,128)}, f32[15,2560]{1,0:T(8,128)}, f32[15,2560]{1,0:T(8,128)}, /*index=5*...) custom-call(f32[15,960]{1,0:T(8,128)} %get-tuple-element.63.refs_0_, ...), custom_call_target="tpu_custom_call" | custom-call | tf_op jit(solution)/shard_map/settle/pallas_call | solution.py:991
  260.1 1.3 slice_bitcast_fusion

commit v2 on v1

--- a/solution.py
+++ b/solution.py
@@ -424,9 +424,9 @@
     c1.s0()
     widen(cot, cp_ref)
     first.s3()
-    c0.s2()
     c1.s1()
     first.s4()
+    c0.s2()
     keep = pltpu.make_async_copy(full, fa, sem.at[0])
     keep.start()
     a_ref = full.reshape(D, NA)
@@ -447,7 +447,7 @@
                 if t < 64 * V_UNIT:
                     v = v * cos_ref[...] + swapped(v) * sin_ref[...]
                 qt_ref[r, t : t + 128] = v.astype(BF16)
-        run({0: [c1.s2]}, i)
+        run({1: [c1.s2]}, i)
         return 0
 
     lax.fori_loop(0, 2, project, 0)
@@ -473,7 +473,7 @@
         for (rows, _), o, stat in zip(jobs, outs, stats):
             ho_ref[rows, tile(p)] = ho_ref[rows, tile(p)] + o.astype(BF16)
             lse[rows, :] = jnp.where(lane == h, stat, lse[rows, :])
-        run({1: [c0.s3], 10: [c1.s3], 12: [c0.s4]}, h)
+        run({4: [c0.s3], 11: [c1.s3], 12: [c0.s4]}, h)
         return 0
 
     lax.fori_loop(0, 15, head, 0)
@@ -576,7 +576,7 @@
         recip = lax.rsqrt(jnp.sum(h * h, axis=1, keepdims=True) * (1.0 / WIDTH) + EPS)
         nrm[r, :] = (h * recip * gain).astype(BF16)
         gacc[r, :] = jnp.zeros((512, D), F32)
-        run({0: [g0.s1, g1.s0], 1: [g0.s2, g1.s1]}, i)
+        run({1: [g0.s1, g1.s0]}, i)
         return 0
 
     lax.fori_loop(0, 2, first, 0)
@@ -593,7 +593,7 @@
         when_chunk(b, 1, "s0_vmem")
         when_chunk(b, 3, "s3")
         when_chunk(b, 4, "s5")
-        run({1: [g0.s4], 2: [g1.s4]}, b)
+        run({0: [g0.s2, g1.s1], 1: [g0.s3, g1.s2], 2: [g1.s3]}, b)
 
         def rows(i, _):
             r = span(i, 512)
@@ -615,7 +615,7 @@
         when_chunk(b, 1, "s1_vmem")
         when_chunk(b, 3, "s4")
 
-        run({0: [g0.s3, g1.s2], 1: [g1.s3]}, b)
+        run({1: [g0.s4], 2: [g1.s4]}, b)
 
         @pl.when(b < BLOCKS - 1)
         def _():
@@ -748,7 +748,6 @@
     loc0, loc1 = scratch[LANDING:k], scratch[k + LANDING : 2 * k]
     scratch = scratch[2 * k :]
     c0.s0()
-    c1.s0()
     get_a = pltpu.make_async_copy(fa, full, isem.at[0])
     get_a.start()
 
@@ -799,7 +798,7 @@
                 dk[g, hi, :] += dk1
                 dq[p, lo, :] += dq0[:256]
                 dq[p, hi, :] += dq0[256:] + dq1
-            run({1: [c0.s1], 3: [c1.s1], 6: [c0.s2], 8: [c0.s3], 9: [c1.s2], 10: [c0.s4], 11: [c1.s3], 12: [c0.s5], 13: [c1.s4]}, h)
+            run({1: [c0.s1, c1.s0], 4: [c1.s1], 8: [c0.s2], 11: [c0.s3, c1.s2], 14: [c0.s4, c1.s3]}, h)
             return 0
 
         lax.fori_loop(0, 15, head, 0)
@@ -819,6 +818,8 @@
             return 0
 
         lax.fori_loop(0, 4, finish, 0)
+        c0.s5()
+        c1.s4()
 
     pl.run_scoped(
         phase_one,
@@ -899,14 +900,13 @@
             mid = (gt - high.astype(F32)).astype(BF16)
             gtok[:, r] = dot_nt(spread[...], high) + dot_nt(spread[...], mid)
             out[:, r] = dot_nt(spread[...], outp[r, :]).astype(BF16)
-            run({0: [d0.s3], 1: [d0.s4], 2: [d1.s2, d0.s5], 3: [d1.s3]}, i)
+            run({0: [d0.s3], 1: [d1.s2, d0.s4], 2: [d1.s3, d0.s5], 3: [d1.s4]}, i)
             return 0
 
         lax.fori_loop(0, 4, tokens, 0)
         puts = [pltpu.make_async_copy(gtok, gtok_hbm, osem.at[0]), pltpu.make_async_copy(out, out_hbm, osem.at[1])]
         for p in puts:
             p.start()
-        d1.s4()
         at = NL
         oo[...] = left[:15, at : at + WIDTH]
         for b in range(BLOCKS):

time: 262 us -> 247 us (0.943)
  Pallas kernels: 258 us -> 244 us
    pallas_call x1, Pallas kernels: 89.6 us -> 79.7 us  [back(): pl.pallas_call(back_kernel, out_shape=[*[shape((15, n), F32) for n in (96...]
    pallas_call x1, Pallas kernels: 66.1 us -> 61.3 us  [attend(): pl.pallas_call(attend_kernel, out_shape=[shape((T, D), BF16), shape((T, D...]
where the time goes in v2:
time: 247 us
  Pallas kernels  244 us (99%)
    pallas_call x1, Pallas kernels, ffn(): pl.pallas_call(ffn_kernel, out_shape=[shape((T, D), F32), shape((T, D), B...  96.4 us
    pallas_call x1, Pallas kernels, back(): pl.pallas_call(back_kernel, out_shape=[*[shape((15, n), F32) for n in (96...  79.7 us
    pallas_call x1, Pallas kernels, attend(): pl.pallas_call(attend_kernel, out_shape=[shape((T, D), BF16), shape((T, D...  61.3 us
    pallas_call x1, Pallas kernels, settle(): pl.pallas_call(settle_kernel, grid=(4,), out_shape=[jax.ShapeDtypeStruct(...  6.11 us

profile of v2, /device:TPU:0, one launch (start us, length us, event | category | flops | bytes accessed | tf_op | source)
XLA Modules:
  0.0 246.7 jit_solution(8160253236825842205)
XLA Ops:
  0.6 1.2 pad_maximum_fusion.gain_ref
  1.8 61.3 %attend.1 = (bf16[1024,1024]{1,0:T(8,128)(2,1)}, bf16[1024,1024]{1,0:T(8,128)(2,1)}, bf16[1024,1024]{1,0:T(8,128)(2,1)}, bf16[1024,1792]{1,0:T(8,128)(2,1)}, bf1...) custom-call(bf16[960,1024]{1,0:T(8,128)(2,1)} %bitcast.14, ...), custom_call_target="tpu_custom_call" | custom-call | tf_op jit(solution)/shard_map/attend/pallas_call | solution.py:499
  63.1 96.4 %ffn.1 = (f32[1024,1024]{1,0:T(8,128)}, bf16[1024,1024]{1,0:T(8,128)(2,1)}, f32[1,1024]{1,0:T(1,128)}, f32[3,16,1536]{2,1,0:T(8,128)}, bf16[1024,1024]{1,0:T(8,1...) custom-call(bf16[1024,1024]{1,0:T(8,128)(2,1)} %get-tuple-element.49, ...), custom_call_target="tpu_custom_call" | custom-call | tf_op jit(solution)/shard_map/ffn/pallas_call | solution.py:698
  159.6 79.7 %back.1 = (f32[15,960]{1,0:T(8,128)}, f32[15,320]{1,0:T(8,128)}, f32[15,320]{1,0:T(8,128)}, f32[15,2560]{1,0:T(8,128)}, f32[15,2560]{1,0:T(8,128)}, /*index=5*/f...) custom-call(bf16[1024,1792]{1,0:T(8,128)(2,1)} %get-tuple-element.47.qt_r, ...), custom_call_target="tpu_custom_call" | custom-call | tf_op jit(solution)/shard_map/back/pallas_call | solution.py:944
  239.3 6.1 %settle.1 = (f32[15,960]{1,0:T(8,128)}, f32[15,320]{1,0:T(8,128)}, f32[15,320]{1,0:T(8,128)}, f32[15,2560]{1,0:T(8,128)}, f32[15,2560]{1,0:T(8,128)}, /*index=5*...) custom-call(f32[15,960]{1,0:T(8,128)} %get-tuple-element.63.refs_0_, ...), custom_call_target="tpu_custom_call" | custom-call | tf_op jit(solution)/shard_map/settle/pallas_call | solution.py:991
  245.4 1.3 slice_bitcast_fusion

commit v3 on v2

--- a/solution.py
+++ b/solution.py
@@ -539,6 +539,8 @@
     loads = [pltpu.make_async_copy(h, v, rsem.at[i]) for i, (h, v) in enumerate(((gate_hbm, gate), (up_hbm, up), (down_hbm, down)))]
     for d in loads:
         d.start()
+    get_b = pltpu.make_async_copy(e0.at[:, :, :, :, :, :NB], b_full, gsem)
+    get_b.start()
     own0[...] = jnp.zeros_like(own0)
     own1[...] = jnp.zeros_like(own1)
     meet()
@@ -550,8 +552,6 @@
     lands, loc = scratch[4 : 4 + LANDING], scratch[4 + LANDING :]
     reduction = lambda j: Scatter(stage, oc_ref.at[j], [ref.at[j] for ref in lands], loc, NC)
     gain = gains[1:2, :]
-    get_b = pltpu.make_async_copy(e0.at[:, :, :, :, :, :NB], b_full, gsem)
-    get_b.start()
 
     def fetch(b, begin):
         slot = jnp.asarray(b) % 2
@@ -576,7 +576,7 @@
         recip = lax.rsqrt(jnp.sum(h * h, axis=1, keepdims=True) * (1.0 / WIDTH) + EPS)
         nrm[r, :] = (h * recip * gain).astype(BF16)
         gacc[r, :] = jnp.zeros((512, D), F32)
-        run({1: [g0.s1, g1.s0]}, i)
+        run({0: [g0.s1, g1.s0], 1: [g0.s2]}, i)
         return 0
 
     lax.fori_loop(0, 2, first, 0)
@@ -593,7 +593,7 @@
         when_chunk(b, 1, "s0_vmem")
         when_chunk(b, 3, "s3")
         when_chunk(b, 4, "s5")
-        run({0: [g0.s2, g1.s1], 1: [g0.s3, g1.s2], 2: [g1.s3]}, b)
+        run({0: [g1.s1], 1: [g0.s3, g1.s2], 2: [g1.s3]}, b)
 
         def rows(i, _):
             r = span(i, 512)

time: 247 us -> 245 us (level)
  no operation moved by 1% of the time
where the time goes in v3:
time: 245 us
  Pallas kernels  242 us (99%)
    pallas_call x1, Pallas kernels, ffn(): pl.pallas_call(ffn_kernel, out_shape=[shape((T, D), F32), shape((T, D), B...  94.5 us
    pallas_call x1, Pallas kernels, back(): pl.pallas_call(back_kernel, out_shape=[*[shape((15, n), F32) for n in (96...  79.7 us
    pallas_call x1, Pallas kernels, attend(): pl.pallas_call(attend_kernel, out_shape=[shape((T, D), BF16), shape((T, D...  61.3 us
    pallas_call x1, Pallas kernels, settle(): pl.pallas_call(settle_kernel, grid=(4,), out_shape=[jax.ShapeDtypeStruct(...  6.11 us

profile of v3, /device:TPU:0, one launch (start us, length us, event | category | flops | bytes accessed | tf_op | source)
XLA Modules:
  0.0 244.7 jit_solution(15504070594355731513)
XLA Ops:
  0.6 1.2 pad_maximum_fusion.gain_ref
  1.8 61.3 %attend.1 = (bf16[1024,1024]{1,0:T(8,128)(2,1)}, bf16[1024,1024]{1,0:T(8,128)(2,1)}, bf16[1024,1024]{1,0:T(8,128)(2,1)}, bf16[1024,1792]{1,0:T(8,128)(2,1)}, bf1...) custom-call(bf16[960,1024]{1,0:T(8,128)(2,1)} %bitcast.14, ...), custom_call_target="tpu_custom_call" | custom-call | tf_op jit(solution)/shard_map/attend/pallas_call | solution.py:499
  63.1 94.5 %ffn.1 = (f32[1024,1024]{1,0:T(8,128)}, bf16[1024,1024]{1,0:T(8,128)(2,1)}, f32[1,1024]{1,0:T(1,128)}, f32[3,16,1536]{2,1,0:T(8,128)}, bf16[1024,1024]{1,0:T(8,1...) custom-call(bf16[1024,1024]{1,0:T(8,128)(2,1)} %get-tuple-element.49, ...), custom_call_target="tpu_custom_call" | custom-call | tf_op jit(solution)/shard_map/ffn/pallas_call | solution.py:698
  157.6 79.7 %back.1 = (f32[15,960]{1,0:T(8,128)}, f32[15,320]{1,0:T(8,128)}, f32[15,320]{1,0:T(8,128)}, f32[15,2560]{1,0:T(8,128)}, f32[15,2560]{1,0:T(8,128)}, /*index=5*/f...) custom-call(bf16[1024,1792]{1,0:T(8,128)(2,1)} %get-tuple-element.47.qt_r, ...), custom_call_target="tpu_custom_call" | custom-call | tf_op jit(solution)/shard_map/back/pallas_call | solution.py:944
  237.3 6.1 %settle.1 = (f32[15,960]{1,0:T(8,128)}, f32[15,320]{1,0:T(8,128)}, f32[15,320]{1,0:T(8,128)}, f32[15,2560]{1,0:T(8,128)}, f32[15,2560]{1,0:T(8,128)}, /*index=5*...) custom-call(f32[15,960]{1,0:T(8,128)} %get-tuple-element.63.refs_0_, ...), custom_call_target="tpu_custom_call" | custom-call | tf_op jit(solution)/shard_map/settle/pallas_call | solution.py:991
  243.4 1.3 slice_bitcast_fusion
